TPU v7x, 32 devices: a whole 2x2x4 slice. The times are simulated.
32 devices in a mesh: leaf: 2 (over y), user: 4 (over x, core), tensor: 4 (over z).
Axes of the slice: x: 2, y: 2, z: 4, core: 2. Of those that a mesh axis runs over, the one named last changes fastest.
Arguments:
- user_feat: bfloat16 [32, 128], P('user'), may hold values from -6 to 6
- beam_nodes: int32 [32, 128], P('user', ('leaf', 'tensor')), may hold values from 0 to 16383, as said below
- item_ids: int32 [32, 384], P('user', 'leaf'), may hold values from 0 to 16383, as said below
- subtree_slot: int32 [32], replicated, may hold values from 0 to 31, as said below
- node_table: bfloat16 [16384, 128], P(('leaf', 'tensor')), may hold values from -6 to 6
- item_table: bfloat16 [16384, 128], P(('leaf', 'tensor')), may hold values from -6 to 6
- mlp_user: bfloat16 [128, 1024], replicated, may hold values from -0.375 to 0.375
- mlp_node: bfloat16 [128, 1024], replicated, may hold values from -0.375 to 0.375
- mlp_bias: float32 [1024], replicated, may hold values from -3 to 3
- mlp_out: bfloat16 [1024], replicated, may hold values from -0.1875 to 0.1875
- proj_in: bfloat16 [384, 2048], P(None, 'tensor'), may hold values from -0.3125 to 0.3125
- cross_w: bfloat16 [2, 2048, 2048], P(None, None, 'tensor'), may hold values from -0.125 to 0.125
- cross_b: float32 [2, 2048], P(None, 'tensor'), may hold values from -3 to 3
- out_w: bfloat16 [2048], P('tensor'), may hold values from -0.125 to 0.125
Outputs:
- beam_score: float32 [32, 128], P('user', ('leaf', 'tensor'))
- interest: float32 [32, 128], P('user')
- logit: float32 [32, 384], P('user', 'leaf')
Inputs may be any that keep to these rules, and one draw needn't show every extreme that they name: A permutation of the subtrees: subtree s is held by index subtree_slot[s] // 4 of leaf+tensor (leaf-major), as its block subtree_slot[s] % 4. `beam_nodes`: within the 8 x 16 block of one device, at most 16 nodes belong to subtrees held by any one index of leaf+tensor; some index receives exactly 16 from every device's block. `item_ids`: split a device's 8 x 192 block, flattened user by user, into 4 runs of 384 items; each run has at most 48 items of subtrees held by any one index of leaf+tensor, and some index receives exactly 48 from every run.
All inputs are finite; a program needn't handle non-finite values.
Results may differ from a plain program's by a relative error of at most 0.0062.
Values may be sent and summed in bfloat16 or wider, within the bound.
A program may use at most 64 MiB of HBM per device.

v0:
```python
import math
import jax
import jax.numpy as jnp
from jax import lax
from jax.sharding import PartitionSpec as P

LAYERS = 2
SUB_NODES = 512
SUB_ITEMS = 512


def small_lookup(table, index):
    hits = index[:, None] == jnp.arange(table.shape[0], dtype=jnp.int32)[None, :]
    return jnp.sum(jnp.where(hits, table[None, :], 0), axis=1)


def bucket_slots(owner, owners, capacity):
    marks = (owner[:, None] == jnp.arange(owners, dtype=jnp.int32)[None, :]).astype(jnp.int32)
    before = jnp.cumsum(marks, axis=0) - marks
    rank = jnp.sum(before * marks, axis=1)
    return owner * capacity + rank


def place_ids(values, dest, total):
    return jnp.full((total,), -1, jnp.int32).at[dest].set(values)


def table_rows(table, wanted):
    found = table[jnp.clip(wanted, 0, None)]
    return jnp.where((wanted >= 0)[..., None], found, jnp.zeros_like(found))


def node_scores(user_rows, node_rows, mlp_node, mlp_bias, mlp_out):
    pre = user_rows + jnp.dot(node_rows, mlp_node, preferred_element_type=jnp.float32) + mlp_bias
    hidden = jax.nn.silu(pre).astype(jnp.bfloat16)
    return jnp.dot(hidden, mlp_out, preferred_element_type=jnp.float32)


def fetch_items(wanted_ids, capacity, owners, subtree_slot, item_table):
    sub_count = item_table.shape[0] // SUB_ITEMS
    slot = small_lookup(subtree_slot, wanted_ids // SUB_ITEMS)
    owner = slot // sub_count
    local = slot % sub_count * SUB_ITEMS + wanted_ids % SUB_ITEMS
    dest = bucket_slots(owner, owners, capacity)
    send = place_ids(local, dest, owners * capacity).reshape(owners, capacity)
    arrived = lax.all_to_all(
        table_rows(
            item_table,
            lax.all_to_all(send, ("leaf", "tensor"), split_axis=0, concat_axis=0, tiled=True),
        ),
        ("leaf", "tensor"),
        split_axis=0,
        concat_axis=0,
        tiled=True,
    )
    return arrived.reshape(owners * capacity, -1)[dest]


def per_device(
    user_feat,
    beam_nodes,
    item_ids,
    subtree_slot,
    node_table,
    item_table,
    mlp_user,
    mlp_node,
    mlp_bias,
    mlp_out,
    proj_in,
    cross_w,
    cross_b,
    out_w,
):
    leaf_count = lax.axis_size("leaf")
    tensor_count = lax.axis_size("tensor")
    owners = leaf_count * tensor_count
    users_here, beam_here = beam_nodes.shape
    requests = users_here * beam_here
    beam_cap = max(2, -(-requests // owners))
    sub_count = node_table.shape[0] // SUB_NODES
    flat_nodes = beam_nodes.reshape(-1)
    node_slot = small_lookup(subtree_slot, flat_nodes // SUB_NODES)
    node_owner = node_slot // sub_count
    node_local = node_slot % sub_count * SUB_NODES + flat_nodes % SUB_NODES
    node_dest = bucket_slots(node_owner, owners, beam_cap)
    node_send = place_ids(node_local, node_dest, owners * beam_cap).reshape(owners, beam_cap)
    user_part = jnp.dot(user_feat, mlp_user, preferred_element_type=jnp.float32)
    request_user = jnp.arange(requests, dtype=jnp.int32) // beam_here
    arrived = lax.all_to_all(
        table_rows(
            node_table,
            lax.all_to_all(node_send, ("leaf", "tensor"), split_axis=0, concat_axis=0, tiled=True),
        ),
        ("leaf", "tensor"),
        split_axis=0,
        concat_axis=0,
        tiled=True,
    )
    node_rows = arrived.reshape(owners * beam_cap, -1)[node_dest]
    scores = node_scores(user_part[request_user], node_rows, mlp_node, mlp_bias, mlp_out)
    weighted = jax.nn.sigmoid(scores)[:, None] * node_rows.astype(jnp.float32)
    numerator = jnp.sum(weighted.reshape(users_here, beam_here, -1), axis=1)
    interest_total = lax.psum(numerator, ("leaf", "tensor"))
    interest = interest_total / math.sqrt(owners * beam_here)
    beam_score = scores.reshape(users_here, beam_here)
    items_here = item_ids.shape[1]
    rows = users_here * items_here
    fetch = rows // tensor_count
    item_cap = max(2, -(-fetch // owners))
    flat_items = item_ids.reshape(-1)
    start = lax.axis_index("tensor") * fetch
    rotated = jnp.roll(flat_items, -start)
    rotated_rows = fetch_items(rotated, tensor_count * item_cap, owners, subtree_slot, item_table)
    item_vec = jnp.roll(rotated_rows, start, axis=0)
    interest_b = interest.astype(jnp.bfloat16)
    user_cols = jnp.repeat(user_feat, items_here, axis=0)
    interest_cols = jnp.repeat(interest_b, items_here, axis=0)
    inputs = jnp.concatenate([user_cols, interest_cols, item_vec], axis=1)
    x_first = jnp.dot(inputs, proj_in, preferred_element_type=jnp.float32).astype(jnp.bfloat16)
    first_wide = x_first.astype(jnp.float32)
    x_now = x_first
    for layer in range(LAYERS):
        weight = cross_w[layer]
        mixed = jnp.dot(
            lax.all_gather(x_now, "tensor", axis=1, tiled=True),
            weight,
            preferred_element_type=jnp.float32,
        )
        x_now = (first_wide * (mixed + cross_b[layer]) + x_now.astype(jnp.float32)).astype(
            jnp.bfloat16
        )
    partial_logit = jnp.dot(x_now, out_w, preferred_element_type=jnp.float32)
    logit = lax.psum(partial_logit, "tensor").reshape(users_here, items_here)
    return (beam_score, interest, logit)


def solution(mesh):
    placed = (
        P("user", None),
        P("user", ("leaf", "tensor")),
        P("user", "leaf"),
        P(),
        P(("leaf", "tensor"), None),
        P(("leaf", "tensor"), None),
        P(),
        P(),
        P(),
        P(),
        P(None, "tensor"),
        P(None, None, "tensor"),
        P(None, "tensor"),
        P("tensor"),
    )
    return jax.shard_map(
        per_device,
        mesh=mesh,
        in_specs=placed,
        out_specs=(P("user", ("leaf", "tensor")), P("user", None), P("user", "leaf")),
        check_vma=False,
    )
```

profile of v0, /device:TPU:0, one launch (start us, length us, event | category | flops | bytes accessed | tf_op | source)
XLA Modules:
  0.0 349.3 jit_solution(13803340638671157353)
XLA Ops:
  7.2 0.9 reshape.317
  9.3 1.0 scatter_custom_fusion
  10.9 7.3 %all-to-all-start = ((s32[8,1,16]{2,1,0:T(1,128)}), s32[8,1,16]{2,1,0:T(1,128)S(1)}, u32[]{:S(2)}, u32[]{:S(2)}) async-start(s32[8,1,16]{2,1,0:T(1,128)} %bitcast.4), calls=%async_computation | async-start | bytes 8192 | tf_op jit(solution)/shard_map/all_to_all | solution.py:93
  18.2 0.8 reshape.322
  20.0 2.3 reduce-window.6
  23.0 1.1 fusion.51
  24.1 6.2 %scatter_custom_fusion.1 = s32[1536]{0:T(1024)S(1)} fusion(s32[1536]{0:T(1024)S(1)} %fusion.36, s32[1536]{0:T(1024)S(1)} %get-tuple-element.5, s32[]{:T(128)} %constant.148.clone.1), kind=kCustom, calls=%fused_computation.98 | custom fusion | bytes 6148 | tf_op jit(solution)/shard_map/scatter | solution.py:25
  31.7 0.8 gather_fusion
  32.5 6.1 %all-to-all-start.2 = ((s32[8,1,192]{2,1,0:T(1,128)}), s32[8,1,192]{2,1,0:T(1,128)S(1)}, u32[]{:S(2)}, u32[]{:S(2)}) async-start(s32[8,1,192]{2,1,0:T(1,128)} %all_to_all.21), calls=%async_computation.2 | async-start | bytes 16384 | tf_op jit(solution)/shard_map/all_to_all | solution.py:49
  40.1 5.0 %all-to-all-done.2 = s32[8,1,192]{2,1,0:T(1,128)S(1)} async-done(((s32[8,1,192]{2,1,0:T(1,128)}), s32[8,1,192]{2,1,0:T(1,128)S(1)}, u32[]{:S(2)}, u32[]{:S(2)}) %all-to-all-start.2) | async-done | bytes 6176 | tf_op jit(solution)/shard_map/all_to_all | solution.py:49
  45.2 3.3 all-to-all-start.1
  48.6 3.2 gather_fusion.3
  51.8 1.0 broadcast_select_fusion
  52.8 2.3 all-to-all-done.1
  55.2 3.6 %all-to-all-start.3 = ((bf16[8,192,128]{2,1,0:T(8,128)(2,1)}), bf16[8,192,128]{2,1,0:T(8,128)(2,1)S(1)}, u32[]{:S(2)}, u32[]{:S(2)}) async-start(bf16[8,192,128]{2,1,0:T(8,128)(2,1)} %broadcast_select_fusion), calls=%async_computation.3 | async-start | bytes 786432 | tf_op jit(solution)/shard_map/all_to_all | solution.py:46
  60.2 21.9 %psum.14 = f32[8,128]{1,0:T(8,128)S(1)} all-reduce(f32[8,128]{1,0:T(8,128)S(1)} %fusion.22), channel_id=1, replica_groups=mesh['leaf'=2,'user'=4,'tensor'=4] {'leaf','tensor'}, use_global_device_ids=true, to_apply=%region_5.6 | all-reduce | flops 1024 | bytes 8192 | tf_op jit(solution)/shard_map/psum | solution.py:104
  82.7 3.2 gather_fusion.4
  85.9 1.5 fusion.19
  87.6 2.1 convolution_convert_fusion
  90.0 112.5 %all-gather.3.cloned.1.call-done = bf16[1536,2048]{1,0:T(8,128)(2,1)} async-done(((bf16[1536,512]{1,0:T(8,128)(2,1)}), bf16[1536,2048]{1,0:T(8,128)(2,1)}) %all-gather.3.cloned.1.call-update) | async-done | bytes 6291472 | tf_op jit(solution)/shard_map/all_gather | solution.py:126
  202.5 8.8 %fusion.1 = bf16[1536,512]{1,0:T(8,128)(2,1)} fusion(bf16[1536,512]{1,0:T(8,128)(2,1)} %convolution_convert_fusion, bf16[1536,2048]{1,0:T(8,128)(2,1)} %all-gather.3.cloned.1.call-done, bf16[2,2048,512]{2,1,0:T(8,128)(2,1)} %param.25, f32[512]{0:T(512)S(1)} %bitcast.106), kind=kOutput, calls=%fused_computation.12 | convolution fusion | flops 3225157632 | bytes 11536384 | tf_op jit(solution)/shard_map/dot_general | solution.py:125
  212.0 113.0 %all-gather.5.cloned.1.call-done = bf16[1536,2048]{1,0:T(8,128)(2,1)} async-done(((bf16[1536,512]{1,0:T(8,128)(2,1)}), bf16[1536,2048]{1,0:T(8,128)(2,1)}) %all-gather.5.cloned.1.call-update) | async-done | bytes 6291472 | tf_op jit(solution)/shard_map/all_gather | solution.py:126
  325.0 8.0 %fusion.16 = f32[1536]{0:T(1024)S(1)} fusion(bf16[512,1]{0,1:T(2,128)(2,1)S(1)} %reshape.389, bf16[1536,512]{1,0:T(8,128)(2,1)} %fusion.1, bf16[1536,2048]{1,0:T(8,128)(2,1)} %all-gather.5.cloned.1.call-done, bf16[1536,512]{1,0:T(8,128)(2,1)S(1)} %copy-done.1, bf16[2,2048,512]{2,1,0:T(8,128)(2,1)} %param.25, f32[512]{0:T(512)S(1)} %bitcast.105), kind=kOutput, calls=%fused_computation.27 | convolution fusion | flops 3227516928 | bytes 11543552 | tf_op jit(solution)/shard_map/dot_general | solution.py:133
  333.1 9.3 %psum.15 = f32[8,192]{1,0:T(8,128)} all-reduce(f32[8,192]{1,0:T(8,128)S(1)} %reshape.325), channel_id=1, replica_groups=mesh['leaf'=2,'user'=4,'tensor'=4] {'tensor'}, use_global_device_ids=true, to_apply=%region_11.12 | all-reduce | flops 1536 | bytes 12288 | tf_op jit(solution)/shard_map/psum | solution.py:134
  (68 shorter events, 9.6 us)
Async XLA Ops:
  7.2 41.4 %copy-start = (bf16[2048,128]{1,0:T(8,128)(2,1)S(1)}, bf16[2048,128]{1,0:T(8,128)(2,1)}, u32[]{:S(2)}) copy-start(bf16[2048,128]{1,0:T(8,128)(2,1)} %param.19) | copy-start | bytes 1572868
  7.2 31.6 %copy-start.2 = (bf16[2048,128]{1,0:T(8,128)(2,1)S(1)}, bf16[2048,128]{1,0:T(8,128)(2,1)}, u32[]{:S(2)}) copy-start(bf16[2048,128]{1,0:T(8,128)(2,1)} %param.18) | copy-start | bytes 1572868
  10.9 21.5 %all-to-all-start = ((s32[8,1,16]{2,1,0:T(1,128)}), s32[8,1,16]{2,1,0:T(1,128)S(1)}, u32[]{:S(2)}, u32[]{:S(2)}) async-start(s32[8,1,16]{2,1,0:T(1,128)} %bitcast.4), calls=%async_computation | async-start | bytes 8192 | tf_op jit(solution)/shard_map/all_to_all | solution.py:93
  32.5 27.1 %copy-start.7 = (bf16[128,1024]{1,0:T(8,128)(2,1)S(1)}, bf16[128,1024]{1,0:T(8,128)(2,1)}, u32[]{:S(2)}) copy-start(bf16[128,1024]{1,0:T(8,128)(2,1)} %param.21) | copy-start | bytes 786436
  32.5 27.1 %copy-start.8 = (f32[1024]{0:T(1024)S(1)}, f32[1024]{0:T(1024)}, u32[]{:S(2)}) copy-start(f32[1024]{0:T(1024)} %param.22) | copy-start | bytes 12292
  32.5 12.7 %all-to-all-start.2 = ((s32[8,1,192]{2,1,0:T(1,128)}), s32[8,1,192]{2,1,0:T(1,128)S(1)}, u32[]{:S(2)}, u32[]{:S(2)}) async-start(s32[8,1,192]{2,1,0:T(1,128)} %all_to_all.21), calls=%async_computation.2 | async-start | bytes 16384 | tf_op jit(solution)/shard_map/all_to_all | solution.py:49
  45.2 10.0 %all-to-all-start.1 = ((bf16[8,16,128]{2,1,0:T(8,128)(2,1)}), bf16[8,16,128]{2,1,0:T(8,128)(2,1)S(1)}, u32[]{:S(2)}, u32[]{:S(2)}) async-start(bf16[8,16,128]{2,1,0:T(8,128)(2,1)} %broadcast_select_fusion.1), calls=%async_computation.1 | async-start | bytes 65536 | tf_op jit(solution)/shard_map/all_to_all | solution.py:90
  55.2 27.5 %all-to-all-start.3 = ((bf16[8,192,128]{2,1,0:T(8,128)(2,1)}), bf16[8,192,128]{2,1,0:T(8,128)(2,1)S(1)}, u32[]{:S(2)}, u32[]{:S(2)}) async-start(bf16[8,192,128]{2,1,0:T(8,128)(2,1)} %broadcast_select_fusion), calls=%async_computation.3 | async-start | bytes 786432 | tf_op jit(solution)/shard_map/all_to_all | solution.py:46
  58.8 143.7 %all-gather.3.cloned.1.call-start = ((), (), s32[]{:S(2)}) async-start(), calls=%async_computation.4 | async-start | bytes 7864320 | tf_op jit(solution)/shard_map/all_gather | solution.py:126
  59.6 27.9 %copy-start.3 = (bf16[8,128]{1,0:T(8,128)(2,1)S(1)}, bf16[8,128]{1,0:T(8,128)(2,1)}, u32[]{:S(2)}) copy-start(bf16[8,128]{1,0:T(8,128)(2,1)} %param.14) | copy-start | bytes 6148
  59.9 27.6 %copy-start.6 = (bf16[384,512]{1,0:T(8,128)(2,1)S(1)}, bf16[384,512]{1,0:T(8,128)(2,1)}, u32[]{:S(2)}) copy-start(bf16[384,512]{1,0:T(8,128)(2,1)} %param.24) | copy-start | bytes 1179652
  87.5 2.4 copy-start.4
  89.7 235.3 %all-gather.5.cloned.1.call-start = ((), (), s32[]{:S(2)}) async-start(), calls=%async_computation.5 | async-start | bytes 7864320 | tf_op jit(solution)/shard_map/all_gather | solution.py:126
  202.5 8.9 %copy-start.5 = (bf16[512]{0:T(512)(128)(2,1)S(1)}, bf16[512]{0:T(512)(128)(2,1)}, u32[]{:S(2)}) copy-start(bf16[512]{0:T(512)(128)(2,1)} %param.27) | copy-start | bytes 3076
  202.5 122.5 %copy-start.1 = (bf16[1536,512]{1,0:T(8,128)(2,1)S(1)}, bf16[1536,512]{1,0:T(8,128)(2,1)}, u32[]{:S(2)}) copy-start(bf16[1536,512]{1,0:T(8,128)(2,1)} %convolution_convert_fusion) | copy-start | bytes 4718596
Sparse Core Ops, SparseCore 0:
  89.8 112.5 all-gather.2
  211.4 113.4 all-gather.4
where the time goes:
time: 350 us; the launch traced here: 349 us
  waiting for transfers between devices  233 us (67%)
  blocking collectives  31.2 us (9%)
  local copies, waits for them, and re-layouts  20.9 us (6%)
  starting transfers between devices  20.6 us (6%)
  matrix products  20.5 us (6%)
  between operations  14.4 us (4%)
  other arithmetic  8.75 us (2%)
    all_gather x2, waiting for transfers between devices, per_device(): lax.all_gather(x_now, 'tensor', axis=1, tiled=True)  225 us
    psum x1, blocking collectives, per_device(): interest_total = lax.psum(numerator, ('leaf', 'tensor'))  21.9 us
    psum x1, blocking collectives, per_device(): logit = lax.psum(partial_logit, 'tensor').reshape(users_here, items_here)  9.35 us
    dot_general x1, matrix products, per_device(): jnp.dot(lax.all_gather(x_now, 'tensor', axis=1, tiled=True), weight, pref...  8.83 us
    dot_general x1, matrix products, per_device(): partial_logit = jnp.dot(x_now, out_w, preferred_element_type=jnp.float32)  8.02 us
    all_to_all x1, starting transfers between devices, per_device(): lax.all_to_all(node_send, ('leaf', 'tensor'), split_axis=0, concat_axis=0...  7.31 us
    scatter x2, local copies, waits for them, and re-layouts, place_ids(): return jnp.full((total,), -1, jnp.int32).at[dest].set(values)  7.16 us
  transfers between devices with their start and end apart: 6, of which 4 were waited for; matrix products, arithmetic and copies ran while one was open for 6% of the time, Pallas kernels for 0%

commit v1 on v0

--- a/solution.py
+++ b/solution.py
@@ -7,6 +7,19 @@
 LAYERS = 2
 SUB_NODES = 512
 SUB_ITEMS = 512
+
+
+def ring_gather(x, axis, dim):
+    length, position, width = (lax.axis_size(axis), lax.axis_index(axis), x.shape[dim])
+    upward = [(i, (i + 1) % length) for i in range(length)]
+    out = jnp.zeros((*x.shape[:dim], length * width, *x.shape[dim + 1 :]), x.dtype)
+    current = x
+    for step in range(length):
+        owner = (position - step) % length
+        out = lax.dynamic_update_slice_in_dim(out, current, owner * width, axis=dim)
+        if step < length - 1:
+            current = lax.ppermute(current, axis, upward)
+    return out
 
 
 def small_lookup(table, index):
@@ -122,11 +135,7 @@
     x_now = x_first
     for layer in range(LAYERS):
         weight = cross_w[layer]
-        mixed = jnp.dot(
-            lax.all_gather(x_now, "tensor", axis=1, tiled=True),
-            weight,
-            preferred_element_type=jnp.float32,
-        )
+        mixed = jnp.dot(ring_gather(x_now, "tensor", 1), weight, preferred_element_type=jnp.float32)
         x_now = (first_wide * (mixed + cross_b[layer]) + x_now.astype(jnp.float32)).astype(
             jnp.bfloat16
         )

time: 350 us -> 319 us (0.911)
  waiting for transfers between devices: 233 us -> 195 us
  local copies, waits for them, and re-layouts: 20.9 us -> 42.8 us
  between operations: 14.4 us -> 1 us
    all_gather x2 -> x0, waiting for transfers between devices: 225 us -> none  [per_device(): lax.all_gather(x_now, 'tensor', axis=1, tiled=True)]
    ppermute x0 -> x6, waiting for transfers between devices: none -> 187 us  [ring_gather(): current = lax.ppermute(current, axis, upward)]
    dynamic_update_slice x0 -> x6, local copies, waits for them, and re-layouts: none -> 13.5 us  [ring_gather(): out = lax.dynamic_update_slice_in_dim(out, current, owner * width, axis=dim)]
    another operation x0 -> x2, local copies, waits for them, and re-layouts: none -> 7.44 us
  transfers between devices with their start and end apart: 6 -> 10, of which waited for: 4 -> 8; matrix products, arithmetic and copies ran while one was open for 6% -> 9% of each run, Pallas kernels for 0% -> 0%
where the time goes in v1:
time: 319 us; the launch traced here: 318 us
  waiting for transfers between devices  195 us (61%)
  local copies, waits for them, and re-layouts  42.8 us (13%)
  blocking collectives  31 us (10%)
  starting transfers between devices  20.4 us (6%)
  matrix products  19.6 us (6%)
  other arithmetic  8.76 us (3%)
    ppermute x6, waiting for transfers between devices, ring_gather(): current = lax.ppermute(current, axis, upward)  187 us
    psum x1, blocking collectives, per_device(): interest_total = lax.psum(numerator, ('leaf', 'tensor'))  21.9 us
    dynamic_update_slice x6, local copies, waits for them, and re-layouts, ring_gather(): out = lax.dynamic_update_slice_in_dim(out, current, owner * width, axis=dim)  13.5 us
    psum x1, blocking collectives, per_device(): logit = lax.psum(partial_logit, 'tensor').reshape(users_here, items_here)  9.07 us
    dot_general x1, matrix products, per_device(): partial_logit = jnp.dot(x_now, out_w, preferred_element_type=jnp.float32)  8.35 us
    dot_general x1, matrix products, per_device(): jnp.dot(ring_gather(x_now, 'tensor', 1), weight, preferred_element_type=j...  7.6 us
    another operation x2, local copies, waits for them, and re-layouts  7.44 us
    all_to_all x1, starting transfers between devices, per_device(): lax.all_to_all(node_send, ('leaf', 'tensor'), split_axis=0, concat_axis=0...  7.31 us
  transfers between devices with their start and end apart: 10, of which 8 were waited for; matrix products, arithmetic and copies ran while one was open for 9% of the time, Pallas kernels for 0%

profile of v1, /device:TPU:0, one launch (start us, length us, event | category | flops | bytes accessed | tf_op | source)
XLA Modules:
  0.0 318.2 jit_solution(1009153295056977786)
XLA Ops:
  4.4 7.3 %all-to-all-start = ((s32[8,1,16]{2,1,0:T(1,128)}), s32[8,1,16]{2,1,0:T(1,128)S(1)}, u32[]{:S(2)}, u32[]{:S(2)}) async-start(s32[8,1,16]{2,1,0:T(1,128)} %bitcast.4), calls=%async_computation | async-start | bytes 8192 | tf_op jit(solution)/shard_map/all_to_all | solution.py:106
  17.6 6.2 %scatter_custom_fusion.1 = s32[1536]{0:T(1024)S(1)} fusion(s32[1536]{0:T(1024)S(1)} %fusion.36, s32[1536]{0:T(1024)S(1)} %get-tuple-element.5, s32[]{:T(128)} %constant.182.clone.1), kind=kCustom, calls=%fused_computation.98 | custom fusion | bytes 6148 | tf_op jit(solution)/shard_map/scatter | solution.py:38
  26.0 6.1 %all-to-all-start.2 = ((s32[8,1,192]{2,1,0:T(1,128)}), s32[8,1,192]{2,1,0:T(1,128)S(1)}, u32[]{:S(2)}, u32[]{:S(2)}) async-start(s32[8,1,192]{2,1,0:T(1,128)} %all_to_all.21), calls=%async_computation.2 | async-start | bytes 16384 | tf_op jit(solution)/shard_map/all_to_all | solution.py:62
  33.6 5.0 %all-to-all-done.2 = s32[8,1,192]{2,1,0:T(1,128)S(1)} async-done(((s32[8,1,192]{2,1,0:T(1,128)}), s32[8,1,192]{2,1,0:T(1,128)S(1)}, u32[]{:S(2)}, u32[]{:S(2)}) %all-to-all-start.2) | async-done | bytes 6176 | tf_op jit(solution)/shard_map/all_to_all | solution.py:62
  38.7 3.3 %all-to-all-start.1 = ((bf16[8,16,128]{2,1,0:T(8,128)(2,1)}), bf16[8,16,128]{2,1,0:T(8,128)(2,1)S(1)}, u32[]{:S(2)}, u32[]{:S(2)}) async-start(bf16[8,16,128]{2,1,0:T(8,128)(2,1)} %broadcast_select_fusion.1), calls=%async_computation.1 | async-start | bytes 65536 | tf_op jit(solution)/shard_map/all_to_all | solution.py:103
  42.1 3.2 %gather_fusion.3 = bf16[1536,128]{1,0:T(8,128)(2,1)S(1)} fusion(bf16[2048,128]{1,0:T(8,128)(2,1)S(1)} %copy-done, s32[2048]{0:T(1024)S(1)} %pad_clamp_fusion.1), kind=kCustom, calls=%fused_computation.3 | custom fusion | bytes 792576 | tf_op jit(solution)/shard_map/gather | solution.py:42
  48.7 3.6 %all-to-all-start.3 = ((bf16[8,192,128]{2,1,0:T(8,128)(2,1)}), bf16[8,192,128]{2,1,0:T(8,128)(2,1)S(1)}, u32[]{:S(2)}, u32[]{:S(2)}) async-start(bf16[8,192,128]{2,1,0:T(8,128)(2,1)} %broadcast_select_fusion), calls=%async_computation.3 | async-start | bytes 786432 | tf_op jit(solution)/shard_map/all_to_all | solution.py:59
  53.6 21.9 %psum.14 = f32[8,128]{1,0:T(8,128)S(1)} all-reduce(f32[8,128]{1,0:T(8,128)S(1)} %fusion.22), channel_id=1, replica_groups=mesh['leaf'=2,'user'=4,'tensor'=4] {'leaf','tensor'}, use_global_device_ids=true, to_apply=%region_5.6 | all-reduce | flops 1024 | bytes 8192 | tf_op jit(solution)/shard_map/psum | solution.py:117
  76.2 3.2 %gather_fusion.4 = bf16[1536,128]{1,0:T(8,128)(2,1)S(1)} fusion(bf16[1536,128]{1,0:T(8,128)(2,1)S(1)} %bitcast.98, s32[2048]{0:T(1024)S(1)} %pad_clamp_fusion), kind=kCustom, calls=%fused_computation.4 | custom fusion | bytes 792576 | tf_op jit(solution)/shard_map/gather | solution.py:69
  81.0 3.5 %broadcast.396.clone = bf16[1536,2048]{1,0:T(8,128)(2,1)} broadcast(bf16[]{:T(256)} %constant.191.clone.1), dimensions={} | broadcast | bytes 6291458 | tf_op jit(solution)/shard_map/broadcast.14
  86.7 34.6 %collective-permute-done = bf16[1536,512]{1,0:T(8,128)(2,1)S(1)} collective-permute-done((bf16[1536,512]{1,0:T(8,128)(2,1)S(1)}, bf16[1536,512]{1,0:T(8,128)(2,1)S(1)}, u32[]{:S(2)}, u32[]{:S(2)}) %collective-permute-start) | collective-permute-done | bytes 1572896 | tf_op jit(solution)/shard_map/ppermute | solution.py:21
  121.2 34.3 %collective-permute-done.1 = bf16[1536,512]{1,0:T(8,128)(2,1)} collective-permute-done((bf16[1536,512]{1,0:T(8,128)(2,1)S(1)}, bf16[1536,512]{1,0:T(8,128)(2,1)}, u32[]{:S(2)}, u32[]{:S(2)}) %collective-permute-start.1) | collective-permute-done | bytes 1572896 | tf_op jit(solution)/shard_map/ppermute | solution.py:21
  156.9 2.7 constant_dynamic-update-slice_fusion.4
  159.7 26.3 %collective-permute-done.2 = bf16[1536,512]{1,0:T(8,128)(2,1)} collective-permute-done((bf16[1536,512]{1,0:T(8,128)(2,1)}, bf16[1536,512]{1,0:T(8,128)(2,1)}, u32[]{:S(2)}, u32[]{:S(2)}) %collective-permute-start.2) | collective-permute-done | bytes 1572896 | tf_op jit(solution)/shard_map/ppermute | solution.py:21
  186.0 2.7 constant_dynamic-update-slice_fusion.3
  188.7 4.0 %broadcast.396 = bf16[1536,2048]{1,0:T(8,128)(2,1)} broadcast(bf16[]{:T(256)} %constant.191.clone.1), dimensions={} | broadcast | bytes 6291458 | tf_op jit(solution)/shard_map/broadcast.14
  193.6 7.6 %constant_dynamic-update-slice_fusion.2 = (bf16[1536,2048]{1,0:T(8,128)(2,1)}, bf16[1536,512]{1,0:T(8,128)(2,1)S(1)}) fusion(bf16[1536,2048]{1,0:T(8,128)(2,1)} %broadcast.396, s32[]{:T(128)S(6)} %select_n.216, f32[512]{0:T(512)S(1)} %bitcast.108, bf16[1536,2048]{1,0:T(8,128)(2,1)} %constant_dynamic-update-slice_fusion.3, ...), kind=kOutput, calls=%fused_computation.105 | convolution fusion | flops 3225157632 | bytes 13109252 | tf_op jit(solution)/shard_map/dot_general | solution.py:138
  201.2 34.6 %collective-permute-done.3 = bf16[1536,512]{1,0:T(8,128)(2,1)S(1)} collective-permute-done((bf16[1536,512]{1,0:T(8,128)(2,1)S(1)}, bf16[1536,512]{1,0:T(8,128)(2,1)S(1)}, u32[]{:S(2)}, u32[]{:S(2)}) %collective-permute-start.3) | collective-permute-done | bytes 1572896 | tf_op jit(solution)/shard_map/ppermute | solution.py:21
  235.8 34.3 %collective-permute-done.4 = bf16[1536,512]{1,0:T(8,128)(2,1)} collective-permute-done((bf16[1536,512]{1,0:T(8,128)(2,1)S(1)}, bf16[1536,512]{1,0:T(8,128)(2,1)}, u32[]{:S(2)}, u32[]{:S(2)}) %collective-permute-start.4) | collective-permute-done | bytes 1572896 | tf_op jit(solution)/shard_map/ppermute | solution.py:21
  272.1 2.8 constant_dynamic-update-slice_fusion
  274.9 23.1 %collective-permute-done.5 = bf16[1536,512]{1,0:T(8,128)(2,1)} collective-permute-done((bf16[1536,512]{1,0:T(8,128)(2,1)}, bf16[1536,512]{1,0:T(8,128)(2,1)}, u32[]{:S(2)}, u32[]{:S(2)}) %collective-permute-start.5) | collective-permute-done | bytes 1572896 | tf_op jit(solution)/shard_map/ppermute | solution.py:21
  298.0 2.7 constant_dynamic-update-slice_fusion.7
  300.7 8.3 %fusion.16 = f32[1536]{0:T(1024)S(1)} fusion(bf16[512,1]{0,1:T(2,128)(2,1)S(1)} %reshape.389, bf16[1536,512]{1,0:T(8,128)(2,1)} %copy-done.8, bf16[1536,2048]{1,0:T(8,128)(2,1)} %constant_dynamic-update-slice_fusion.7, bf16[1536,512]{1,0:T(8,128)(2,1)} %copy-done.6, bf16[2,2048,512]{2,1,0:T(8,128)(2,1)} %param.25, f32[512]{0:T(512)S(1)} %bitcast.107), kind=kOutput, calls=%fused_computation.27 | convolution fusion | flops 3227516928 | bytes 11543552 | tf_op jit(solution)/shard_map/dot_general | solution.py:142
  309.1 9.1 %psum.15 = f32[8,192]{1,0:T(8,128)} all-reduce(f32[8,192]{1,0:T(8,128)S(1)} %reshape.325), channel_id=1, replica_groups=mesh['leaf'=2,'user'=4,'tensor'=4] {'tensor'}, use_global_device_ids=true, to_apply=%region_11.12 | all-reduce | flops 1536 | bytes 12288 | tf_op jit(solution)/shard_map/psum | solution.py:143
  (88 shorter events, 26.7 us)
Async XLA Ops:
  0.6 41.5 %copy-start = (bf16[2048,128]{1,0:T(8,128)(2,1)S(1)}, bf16[2048,128]{1,0:T(8,128)(2,1)}, u32[]{:S(2)}) copy-start(bf16[2048,128]{1,0:T(8,128)(2,1)} %param.19) | copy-start | bytes 1572868
  0.6 31.6 %copy-start.1 = (bf16[2048,128]{1,0:T(8,128)(2,1)S(1)}, bf16[2048,128]{1,0:T(8,128)(2,1)}, u32[]{:S(2)}) copy-start(bf16[2048,128]{1,0:T(8,128)(2,1)} %param.18) | copy-start | bytes 1572868
  4.4 21.6 %all-to-all-start = ((s32[8,1,16]{2,1,0:T(1,128)}), s32[8,1,16]{2,1,0:T(1,128)S(1)}, u32[]{:S(2)}, u32[]{:S(2)}) async-start(s32[8,1,16]{2,1,0:T(1,128)} %bitcast.4), calls=%async_computation | async-start | bytes 8192 | tf_op jit(solution)/shard_map/all_to_all | solution.py:106
  25.9 27.0 %copy-start.10 = (bf16[128,1024]{1,0:T(8,128)(2,1)S(1)}, bf16[128,1024]{1,0:T(8,128)(2,1)}, u32[]{:S(2)}) copy-start(bf16[128,1024]{1,0:T(8,128)(2,1)} %param.21) | copy-start | bytes 786436
  26.0 27.0 %copy-start.11 = (f32[1024]{0:T(1024)S(1)}, f32[1024]{0:T(1024)}, u32[]{:S(2)}) copy-start(f32[1024]{0:T(1024)} %param.22) | copy-start | bytes 12292
  26.0 12.7 %all-to-all-start.2 = ((s32[8,1,192]{2,1,0:T(1,128)}), s32[8,1,192]{2,1,0:T(1,128)S(1)}, u32[]{:S(2)}, u32[]{:S(2)}) async-start(s32[8,1,192]{2,1,0:T(1,128)} %all_to_all.21), calls=%async_computation.2 | async-start | bytes 16384 | tf_op jit(solution)/shard_map/all_to_all | solution.py:62
  38.7 10.0 %all-to-all-start.1 = ((bf16[8,16,128]{2,1,0:T(8,128)(2,1)}), bf16[8,16,128]{2,1,0:T(8,128)(2,1)S(1)}, u32[]{:S(2)}, u32[]{:S(2)}) async-start(bf16[8,16,128]{2,1,0:T(8,128)(2,1)} %broadcast_select_fusion.1), calls=%async_computation.1 | async-start | bytes 65536 | tf_op jit(solution)/shard_map/all_to_all | solution.py:103
  48.7 27.5 %all-to-all-start.3 = ((bf16[8,192,128]{2,1,0:T(8,128)(2,1)}), bf16[8,192,128]{2,1,0:T(8,128)(2,1)S(1)}, u32[]{:S(2)}, u32[]{:S(2)}) async-start(bf16[8,192,128]{2,1,0:T(8,128)(2,1)} %broadcast_select_fusion), calls=%async_computation.3 | async-start | bytes 786432 | tf_op jit(solution)/shard_map/all_to_all | solution.py:59
  53.0 28.0 %copy-start.2 = (bf16[8,128]{1,0:T(8,128)(2,1)S(1)}, bf16[8,128]{1,0:T(8,128)(2,1)}, u32[]{:S(2)}) copy-start(bf16[8,128]{1,0:T(8,128)(2,1)} %param.14) | copy-start | bytes 6148
  81.0 3.5 %copy-start.9 = (bf16[384,512]{1,0:T(8,128)(2,1)S(1)}, bf16[384,512]{1,0:T(8,128)(2,1)}, u32[]{:S(2)}) copy-start(bf16[384,512]{1,0:T(8,128)(2,1)} %param.24) | copy-start | bytes 1179652
  84.5 71.1 %copy-start.3 = (f32[2,512]{1,0:T(2,128)S(1)}, f32[2,512]{1,0:T(2,128)}, u32[]{:S(2)}) copy-start(f32[2,512]{1,0:T(2,128)} %param.26) | copy-start | bytes 12292
  86.7 68.9 %copy-start.6 = (bf16[1536,512]{1,0:T(8,128)(2,1)}, bf16[1536,512]{1,0:T(8,128)(2,1)S(1)}, u32[]{:S(2)}) copy-start(bf16[1536,512]{1,0:T(8,128)(2,1)S(1)} %get-tuple-element.14) | copy-start | bytes 4718596
  86.7 34.6 %collective-permute-start = (bf16[1536,512]{1,0:T(8,128)(2,1)S(1)}, bf16[1536,512]{1,0:T(8,128)(2,1)S(1)}, u32[]{:S(2)}, u32[]{:S(2)}) collective-permute-start(bf16[1536,512]{1,0:T(8,128)(2,1)S(1)} %get-tuple-element.14), channel_id=1, source_target_pairs={{0,1},{1,2},{2,3},{3,0},{4,5},{5,6},{6,7},{7,4},{8,9},{9,10},{10,1... | collective-permute-start | bytes 4718600 | tf_op jit(solution)/shard_map/ppermute | solution.py:21
  121.2 34.3 %collective-permute-start.1 = (bf16[1536,512]{1,0:T(8,128)(2,1)S(1)}, bf16[1536,512]{1,0:T(8,128)(2,1)}, u32[]{:S(2)}, u32[]{:S(2)}) collective-permute-start(bf16[1536,512]{1,0:T(8,128)(2,1)S(1)} %collective-permute-done), channel_id=1, source_target_pairs={{0,1},{1,2},{2,3},{3,0},{4,5},{5,6},{6,7},{7,4},{8,9},{9,10},{10,1... | collective-permute-start | bytes 4718600 | tf_op jit(solution)/shard_map/ppermute | solution.py:21
  155.6 30.4 %collective-permute-start.2 = (bf16[1536,512]{1,0:T(8,128)(2,1)}, bf16[1536,512]{1,0:T(8,128)(2,1)}, u32[]{:S(2)}, u32[]{:S(2)}) collective-permute-start(bf16[1536,512]{1,0:T(8,128)(2,1)} %collective-permute-done.1), channel_id=1, source_target_pairs={{0,1},{1,2},{2,3},{3,0},{4,5},{5,6},{6,7},{7,4},{8,9},{9,10},{10,1... | collective-permute-start | bytes 4718600 | tf_op jit(solution)/shard_map/ppermute | solution.py:21
  188.7 4.0 %copy-start.5 = (bf16[2,2048,512]{2,1,0:T(8,128)(2,1)S(1)}, bf16[2,2048,512]{2,1,0:T(8,128)(2,1)}, u32[]{:S(2)}) copy-start(bf16[2,2048,512]{2,1,0:T(8,128)(2,1)} %param.25) | copy-start | bytes 12582916
  188.7 4.9 %copy-start.7 = (bf16[1536,512]{1,0:T(8,128)(2,1)S(1)}, bf16[1536,512]{1,0:T(8,128)(2,1)}, u32[]{:S(2)}) copy-start(bf16[1536,512]{1,0:T(8,128)(2,1)} %copy-done.6) | copy-start | bytes 4718596
  193.6 76.5 %copy-start.4 = (bf16[512]{0:T(512)(128)(2,1)S(1)}, bf16[512]{0:T(512)(128)(2,1)}, u32[]{:S(2)}) copy-start(bf16[512]{0:T(512)(128)(2,1)} %param.27) | copy-start | bytes 3076
  201.2 68.9 %copy-start.8 = (bf16[1536,512]{1,0:T(8,128)(2,1)}, bf16[1536,512]{1,0:T(8,128)(2,1)S(1)}, u32[]{:S(2)}) copy-start(bf16[1536,512]{1,0:T(8,128)(2,1)S(1)} %get-tuple-element.16) | copy-start | bytes 4718596
  201.2 34.6 %collective-permute-start.3 = (bf16[1536,512]{1,0:T(8,128)(2,1)S(1)}, bf16[1536,512]{1,0:T(8,128)(2,1)S(1)}, u32[]{:S(2)}, u32[]{:S(2)}) collective-permute-start(bf16[1536,512]{1,0:T(8,128)(2,1)S(1)} %get-tuple-element.16), channel_id=1, source_target_pairs={{0,1},{1,2},{2,3},{3,0},{4,5},{5,6},{6,7},{7,4},{8,9},{9,10},{10,1... | collective-permute-start | bytes 4718600 | tf_op jit(solution)/shard_map/ppermute | solution.py:21
  235.8 34.3 %collective-permute-start.4 = (bf16[1536,512]{1,0:T(8,128)(2,1)S(1)}, bf16[1536,512]{1,0:T(8,128)(2,1)}, u32[]{:S(2)}, u32[]{:S(2)}) collective-permute-start(bf16[1536,512]{1,0:T(8,128)(2,1)S(1)} %collective-permute-done.3), channel_id=1, source_target_pairs={{0,1},{1,2},{2,3},{3,0},{4,5},{5,6},{6,7},{7,4},{8,9},{9,10},{10,1... | collective-permute-start | bytes 4718600 | tf_op jit(solution)/shard_map/ppermute | solution.py:21
  270.1 27.9 %collective-permute-start.5 = (bf16[1536,512]{1,0:T(8,128)(2,1)}, bf16[1536,512]{1,0:T(8,128)(2,1)}, u32[]{:S(2)}, u32[]{:S(2)}) collective-permute-start(bf16[1536,512]{1,0:T(8,128)(2,1)} %collective-permute-done.4), channel_id=1, source_target_pairs={{0,1},{1,2},{2,3},{3,0},{4,5},{5,6},{6,7},{7,4},{8,9},{9,10},{10,1... | collective-permute-start | bytes 4718600 | tf_op jit(solution)/shard_map/ppermute | solution.py:21
